TPU v7x, 256 devices: a whole 4x4x8 slice. The times are simulated.
256 devices in a mesh: row: 32 (over x, z), col: 8 (over y, core).
Axes of the slice: x: 4, y: 4, z: 8, core: 2. Of those that a mesh axis runs over, the one named last changes fastest.
Arguments:
- momentum: float32 [5120, 13312], P('row', 'col')
- gradient: float32 [5120, 13312], P('row', 'col'), may hold values from -6 to 6
Outputs:
- new_momentum: float32 [5120, 13312], P('row', 'col')
- update: float32 [5120, 13312], P('row', 'col')
All inputs are finite; a program needn't handle non-finite values.
Results may differ from a plain program's by a relative error of at most 0.00073.
The roundings to bfloat16 on the way count: a program that leaves them out, or rounds other values in their place, can miss the bound.
Values may be sent and summed in bfloat16 or wider, within the bound.
A program may use at most 64 MiB of HBM per device.

v0:
```python
import functools
import jax
import jax.numpy as jnp
from jax import lax
from jax.sharding import Mesh
from jax.sharding import PartitionSpec as P

D = 5120
FF_WIN = 13312
ROW_COL = ("row_0", "row_1", "col_0", "col_1")
ROW = ("row_0", "row_1")
COL = ("col_0", "col_1")


def by_axis(array, axes):
    return functools.reduce(lax.psum, axes, array)


def gram_rows(left, right):
    return lax.dot_general(
        left, right, (((1,), (1,)), ((), ())), preferred_element_type=jnp.float32
    )


def shards(momentum, gradient):
    new_momentum = 0.95 * momentum + gradient
    squares = by_axis(jnp.sum(new_momentum * new_momentum), ROW_COL)
    normed = new_momentum / (jnp.sqrt(3.0 * squares / D) + 1e-07)
    rounded = normed.astype(jnp.bfloat16)
    gathered = lax.all_gather(rounded, ROW, axis=0, tiled=True)
    partial_value = gram_rows(rounded, gathered)
    gram = lax.psum(partial_value, COL)
    gram_rounded = gram.astype(jnp.bfloat16)
    product = jnp.dot(gram_rounded, gathered, preferred_element_type=jnp.float32)
    update = (1.5 * normed - 0.5 * product) * jnp.sqrt(jnp.float32(3 * FF_WIN))
    return (new_momentum, update)


def solution(mesh):
    torus = Mesh(mesh.devices.reshape(4, 8, 4, 2), ("row_0", "row_1", "col_0", "col_1"))
    return jax.shard_map(
        shards,
        mesh=torus,
        in_specs=(P(ROW, COL), P(ROW, COL)),
        out_specs=(P(ROW, COL), P(ROW, COL)),
        check_vma=False,
    )
```

profile of v0, /device:TPU:25, one launch (start us, length us, event | category | flops | bytes accessed | tf_op | source)
XLA Modules:
  0.0 273.7 jit_solution(8420792981213836205)
XLA Ops:
  7.2 0.0 all-gather.2.cloned.1.call-start
  7.2 2.4 multiply_reduce_fusion
  9.6 0.0 copy-start
  9.6 9.1 %psum.35 = f32[]{:T(128)} all-reduce(f32[]{:T(128)} %get-tuple-element.2), channel_id=1, replica_groups=mesh['row_0'=4,'row_1'=8,'col_0'=4,'col_1'=2] {'row_0'}, use_global_device_ids=true, to_apply=%region_1.0 | all-reduce | flops 1 | bytes 8 | tf_op jit(solution)/shard_map/psum | solution.py:16
  18.7 16.9 %psum.36 = f32[]{:T(128)} all-reduce(f32[]{:T(128)} %psum.35), channel_id=1, replica_groups=mesh['row_0'=4,'row_1'=8,'col_0'=4,'col_1'=2] {'row_1'}, use_global_device_ids=true, to_apply=%region_2.0 | all-reduce | flops 1 | bytes 8 | tf_op jit(solution)/shard_map/psum | solution.py:16
  35.6 6.4 %psum.37 = f32[]{:T(128)} all-reduce(f32[]{:T(128)} %psum.36), channel_id=1, replica_groups=mesh['row_0'=4,'row_1'=8,'col_0'=4,'col_1'=2] {'col_0'}, use_global_device_ids=true, to_apply=%region_3.0 | all-reduce | flops 1 | bytes 8 | tf_op jit(solution)/shard_map/psum | solution.py:16
  41.9 10.9 %psum.38 = f32[]{:T(128)} all-reduce(f32[]{:T(128)} %psum.37), channel_id=1, replica_groups=mesh['row_0'=4,'row_1'=8,'col_0'=4,'col_1'=2] {'col_1'}, use_global_device_ids=true, to_apply=%region_4.0 | all-reduce | flops 1 | bytes 8 | tf_op jit(solution)/shard_map/psum | solution.py:16
  53.5 0.9 fusion.3
  54.4 0.0 all-gather.2.cloned.1.call-update
  54.4 0.0 copy-done
  54.4 136.6 %all-gather.2.cloned.1.call-done = bf16[5120,1664]{1,0:T(8,128)(2,1)} async-done(((bf16[160,1664]{1,0:T(8,128)(2,1)}), bf16[5120,1664]{1,0:T(8,128)(2,1)}) %all-gather.2.cloned.1.call-update) | async-done | bytes 17039376 | tf_op jit(solution)/shard_map/all_gather | solution.py:30
  191.0 9.3 %fusion.4 = f32[160,5120]{1,0:T(8,128)S(1)} fusion(bf16[160,1664]{1,0:T(8,128)(2,1)} %fusion.3, bf16[5120,1664]{1,0:T(8,128)(2,1)} %all-gather.2.cloned.1.call-done), kind=kOutput, calls=%fused_computation.8 | convolution fusion | flops 2726297600 | bytes 20848640 | tf_op jit(solution)/shard_map/dot_general | solution.py:20
  200.3 55.8 %all-reduce.1 = bf16[160,5120]{1,0:T(8,128)(2,1)} all-reduce(f32[160,5120]{1,0:T(8,128)S(1)} %fusion.4), channel_id=1, replica_groups=mesh['row_0'=4,'row_1'=8,'col_0'=4,'col_1'=2] {'col_0','col_1'}, use_global_device_ids=true, to_apply=%region_5.0 | all-reduce | flops 819200 | bytes 4915200 | tf_op jit(solution)/shard_map/psum | solution.py:32
  256.1 10.8 %fusion.1 = f32[160,1664]{1,0:T(8,128)} fusion(bf16[5120,1664]{1,0:T(8,128)(2,1)} %all-gather.2.cloned.1.call-done, bf16[160,5120]{1,0:T(8,128)(2,1)} %all-reduce.1, f32[160,1664]{1,0:T(8,128)} %copy-done, f32[]{:T(128)S(6)} %add.17), kind=kOutput, calls=%fused_computation.2 | convolution fusion | flops 2727628800 | bytes 20807684 | tf_op jit(solution)/shard_map/dot_general | solution.py:34
Async XLA Ops:
  7.2 183.8 %all-gather.2.cloned.1.call-start = ((), (), s32[]{:S(2)}) async-start(), calls=%async_computation | async-start | bytes 17571840 | tf_op jit(solution)/shard_map/all_gather | solution.py:30
  9.6 44.8 %copy-start = (f32[160,1664]{1,0:T(8,128)}, f32[160,1664]{1,0:T(8,128)S(1)}, u32[]{:S(2)}) copy-start(f32[160,1664]{1,0:T(8,128)S(1)} %get-tuple-element.3) | copy-start | bytes 3194884
Sparse Core Ops, SparseCore 0:
  54.6 136.4 all-gather.1
where the time goes:
time: 274 us
  waiting for transfers between devices  137 us (50%)
  blocking collectives  99 us (36%)
  matrix products  20 us (7%)
  between operations  14.7 us (5%)
  other arithmetic  3.3 us (1%)
    all_gather x1, waiting for transfers between devices, shards(): gathered = lax.all_gather(rounded, ROW, axis=0, tiled=True)  137 us
    psum x1, blocking collectives, shards(): gram = lax.psum(partial_value, COL)  55.8 us
    psum x4, blocking collectives, by_axis(): return functools.reduce(lax.psum, axes, array)  43.2 us
    dot_general x1, matrix products, shards(): jnp.dot(gram_rounded, gathered, preferred_element_type=jnp.float32)  10.8 us
    dot_general x1, matrix products, gram_rows(): lax.dot_general(left, right, (((1,), (1,)), ((), ())), preferred_element_...  9.28 us
  transfers between devices with their start and end apart: 1, of which 1 were waited for; matrix products, arithmetic and copies ran while one was open for 0% of the time, Pallas kernels for 0%

commit v1 on v0

--- a/solution.py
+++ b/solution.py
@@ -29,7 +29,7 @@
     rounded = normed.astype(jnp.bfloat16)
     gathered = lax.all_gather(rounded, ROW, axis=0, tiled=True)
     partial_value = gram_rows(rounded, gathered)
-    gram = lax.psum(partial_value, COL)
+    gram = jnp.sum(lax.all_gather(partial_value, COL), axis=0)
     gram_rounded = gram.astype(jnp.bfloat16)
     product = jnp.dot(gram_rounded, gathered, preferred_element_type=jnp.float32)
     update = (1.5 * normed - 0.5 * product) * jnp.sqrt(jnp.float32(3 * FF_WIN))

time: 274 us -> 358 us (1.31)
  waiting for transfers between devices: 137 us -> 261 us
  blocking collectives: 99 us -> 43.2 us
  other arithmetic: 3.3 us -> 13.4 us
    all_gather x0 -> x1, waiting for transfers between devices: none -> 124 us  [shards(): gram = jnp.sum(lax.all_gather(partial_value, COL), axis=0)]
    psum x1 -> x0, blocking collectives: 55.8 us -> none  [shards(): gram = lax.psum(partial_value, COL)]
    reduce_sum x0 -> x1, other arithmetic: none -> 10.1 us  [shards(): gram = jnp.sum(lax.all_gather(partial_value, COL), axis=0)]
    dot_general x1, matrix products: 9.28 us -> 13.3 us  [gram_rows(): lax.dot_general(left, right, (((1,), (1,)), ((), ())), preferred_element_...]
  transfers between devices with their start and end apart: 1 -> 2, of which waited for: 1 -> 2; matrix products, arithmetic and copies ran while one was open for 0% -> 0% of each run, Pallas kernels for 0% -> 0%
where the time goes in v1:
time: 358 us; the launch traced here: 356 us
  waiting for transfers between devices  261 us (73%)
  blocking collectives  43.2 us (12%)
  matrix products  23.3 us (7%)
  between operations  14.7 us (4%)
  other arithmetic  13.4 us (4%)
    all_gather x1, waiting for transfers between devices, shards(): gathered = lax.all_gather(rounded, ROW, axis=0, tiled=True)  137 us
    all_gather x1, waiting for transfers between devices, shards(): gram = jnp.sum(lax.all_gather(partial_value, COL), axis=0)  124 us
    psum x4, blocking collectives, by_axis(): return functools.reduce(lax.psum, axes, array)  43.2 us
    dot_general x1, matrix products, gram_rows(): lax.dot_general(left, right, (((1,), (1,)), ((), ())), preferred_element_...  13.3 us
    reduce_sum x1, other arithmetic, shards(): gram = jnp.sum(lax.all_gather(partial_value, COL), axis=0)  10.1 us
    dot_general x1, matrix products, shards(): jnp.dot(gram_rounded, gathered, preferred_element_type=jnp.float32)  10 us
  transfers between devices with their start and end apart: 2, of which 2 were waited for; matrix products, arithmetic and copies ran while one was open for 0% of the time, Pallas kernels for 0%

profile of v1, /device:TPU:25, one launch (start us, length us, event | category | flops | bytes accessed | tf_op | source)
XLA Modules:
  0.0 355.7 jit_solution(11252584361960266296)
XLA Ops:
  7.2 0.0 all-gather.4.cloned.1.call-start
  7.2 2.4 multiply_reduce_fusion
  9.6 0.0 copy-start
  9.6 9.1 %psum.28 = f32[]{:T(128)} all-reduce(f32[]{:T(128)} %get-tuple-element.2), channel_id=1, replica_groups=mesh['row_0'=4,'row_1'=8,'col_0'=4,'col_1'=2] {'row_0'}, use_global_device_ids=true, to_apply=%region_1.0 | all-reduce | flops 1 | bytes 8 | tf_op jit(solution)/shard_map/psum | solution.py:16
  18.7 16.9 %psum.29 = f32[]{:T(128)} all-reduce(f32[]{:T(128)} %psum.28), channel_id=1, replica_groups=mesh['row_0'=4,'row_1'=8,'col_0'=4,'col_1'=2] {'row_1'}, use_global_device_ids=true, to_apply=%region_2.0 | all-reduce | flops 1 | bytes 8 | tf_op jit(solution)/shard_map/psum | solution.py:16
  35.6 6.4 %psum.30 = f32[]{:T(128)} all-reduce(f32[]{:T(128)} %psum.29), channel_id=1, replica_groups=mesh['row_0'=4,'row_1'=8,'col_0'=4,'col_1'=2] {'col_0'}, use_global_device_ids=true, to_apply=%region_3.0 | all-reduce | flops 1 | bytes 8 | tf_op jit(solution)/shard_map/psum | solution.py:16
  41.9 10.9 %psum.31 = f32[]{:T(128)} all-reduce(f32[]{:T(128)} %psum.30), channel_id=1, replica_groups=mesh['row_0'=4,'row_1'=8,'col_0'=4,'col_1'=2] {'col_1'}, use_global_device_ids=true, to_apply=%region_4.0 | all-reduce | flops 1 | bytes 8 | tf_op jit(solution)/shard_map/psum | solution.py:16
  53.5 0.9 fusion.3
  54.4 0.0 all-gather.4.cloned.1.call-update
  54.4 0.0 all-gather.6.cloned.1.call-start
  54.5 136.6 %all-gather.4.cloned.1.call-done = bf16[5120,1664]{1,0:T(8,128)(2,1)} async-done(((bf16[160,1664]{1,0:T(8,128)(2,1)}), bf16[5120,1664]{1,0:T(8,128)(2,1)}) %all-gather.4.cloned.1.call-update) | async-done | bytes 17039376 | tf_op jit(solution)/shard_map/all_gather | solution.py:30
  191.0 13.3 %fusion.4 = f32[160,5120]{1,0:T(8,128)} fusion(bf16[160,1664]{1,0:T(8,128)(2,1)} %fusion.3, bf16[5120,1664]{1,0:T(8,128)(2,1)} %all-gather.4.cloned.1.call-done), kind=kOutput, calls=%fused_computation.8 | convolution fusion | flops 2726297600 | bytes 20848640 | tf_op jit(solution)/shard_map/dot_general | solution.py:20
  204.4 0.0 all-gather.6.cloned.1.call-update
  204.4 124.4 %all-gather.6.cloned.1.call-done = f32[1280,5120]{1,0:T(8,128)} async-done(((f32[160,5120]{1,0:T(8,128)}), f32[1280,5120]{1,0:T(8,128)}) %all-gather.6.cloned.1.call-update) | async-done | bytes 26214416 | tf_op jit(solution)/shard_map/all_gather | solution.py:32
  328.8 10.1 %reduce_sum.19 = bf16[160,5120]{1,0:T(8,128)(2,1)S(1)} reduce(f32[8,160,5120]{2,1,0:T(8,128)} %bitcast.5, f32[]{:T(128)} %constant.2.clone.1), dimensions={0}, to_apply=%region_5.0 | reduce | flops 5734400 | bytes 27852804 | tf_op jit(solution)/shard_map/reduce_sum | solution.py:32
  338.9 0.0 copy-done
  338.9 10.0 %fusion.1 = f32[160,1664]{1,0:T(8,128)} fusion(bf16[5120,1664]{1,0:T(8,128)(2,1)} %all-gather.4.cloned.1.call-done, bf16[160,5120]{1,0:T(8,128)(2,1)S(1)} %reduce_sum.19, f32[160,1664]{1,0:T(8,128)S(1)} %get-tuple-element.3, f32[]{:T(128)S(6)} %add.15), kind=kOutput, calls=%fused_computation.2 | convolution fusion | flops 2727628800 | bytes 20807684 | tf_op jit(solution)/shard_map/dot_general | solution.py:34
Async XLA Ops:
  7.2 183.9 %all-gather.4.cloned.1.call-start = ((), (), s32[]{:S(2)}) async-start(), calls=%async_computation | async-start | bytes 17571840 | tf_op jit(solution)/shard_map/all_gather | solution.py:30
  9.6 329.2 %copy-start = (f32[160,1664]{1,0:T(8,128)}, f32[160,1664]{1,0:T(8,128)S(1)}, u32[]{:S(2)}) copy-start(f32[160,1664]{1,0:T(8,128)S(1)} %get-tuple-element.3) | copy-start | bytes 3194884
  54.4 274.4 %all-gather.6.cloned.1.call-start = ((), (), s32[]{:S(2)}) async-start(), calls=%async_computation.1 | async-start | bytes 29491200 | tf_op jit(solution)/shard_map/all_gather | solution.py:32
Sparse Core Ops, SparseCore 0:
  54.6 136.4 all-gather.3
  204.5 124.2 all-gather.5
